TPU v7x, 256 devices: a whole 4x4x8 slice. The times are simulated.
256 devices in a mesh: section: 8 (over z_hi, x), rep: 32 (over z_lo, y, core).
Axes of the slice: x: 4, y: 4, z: 8 (z_hi: 2, z_lo: 4; z = z_hi * 4 + z_lo), core: 2. Of those that a mesh axis runs over, the one named last changes fastest.
Arguments:
- layer_in: bfloat16 [8, 128, 4096], P('section', 'rep'), may hold values from -6 to 6
- next_in: bfloat16 [8, 128, 4096], P('section', 'rep'), may hold values from -6 to 6
- returned: bfloat16 [8, 256, 4096], P('section', 'rep'), may hold values from -6 to 6
- norm_gain: float32 [8, 4096], P('section'), may hold values from 0.25 to 1.75
- gate_weight: bfloat16 [8, 4096, 14336], P('section', None, 'rep'), may hold values from -0.09375 to 0.09375
- up_weight: bfloat16 [8, 4096, 14336], P('section', None, 'rep'), may hold values from -0.09375 to 0.09375
- down_weight: bfloat16 [8, 14336, 4096], P('section', 'rep'), may hold values from -0.046875 to 0.046875
- wiring: int32 [8, 32, 32], P('section'), may hold values from 0 to 2, as said below
Outputs:
- forwarded: bfloat16 [8, 256, 4096], P('section', 'rep')
- input_grad: bfloat16 [8, 128, 4096], P('section', 'rep')
- next_out: bfloat16 [8, 128, 4096], P('section', 'rep')
Inputs may be any that keep to these rules, and one draw needn't show every extreme that they name: For every position p and row group r the entries wiring[p, r, :] sum to 2. For every position p and receiver j the column wiring[p, :, j] sums to at most 4, and in every position some column sums to exactly 4. In every position some row group sends all its 2 blocks to one receiver, and some receiver gets none.
All inputs are finite; a program needn't handle non-finite values.
Results may differ from a plain program's by a relative error of at most 0.035.
Values may be sent and summed in bfloat16 or wider, within the bound.
No kernel may reach another device: no remote copies, remote signals or barrier semaphores. Data moves between devices by JAX's collectives and lax.ppermute only.
A program may use at most 128 MiB of HBM per device.

v0:
```python
import jax
import jax.numpy as jnp
from jax import lax
from jax.sharding import PartitionSpec as P

BLK = 2
epsilon = 1e-05
step_rate = 0.5


def passed_along(value, axis, by):
    peers = lax.axis_size(axis)
    return lax.ppermute(value, axis, [(i, (i + by) % peers) for i in range(peers)])


def route_tables(wiring_section, replicas, blocks_dev, capacity):
    row_total = jnp.cumsum(wiring_section, axis=1)
    column_total = jnp.cumsum(wiring_section, axis=0)
    row_start = row_total - wiring_section
    column_start = column_total - wiring_section
    slot_ids = jnp.arange(capacity, dtype=jnp.int32)
    block_ids = jnp.arange(blocks_dev, dtype=jnp.int32)
    member_ids = jnp.arange(replicas, dtype=jnp.int32)
    sender = jnp.sum(
        (column_total.T[:, :, None] <= slot_ids[None, None, :]).astype(jnp.int32), axis=1
    )
    slot_live = slot_ids[None, :] < column_total[replicas - 1][:, None]
    sender = jnp.minimum(sender, replicas - 1)
    within = slot_ids[None, :] - column_start[sender, member_ids[:, None]]
    within = jnp.where(slot_live, within, 0)
    local_source = sender * blocks_dev + within
    global_source = sender * blocks_dev + row_start[sender, member_ids[:, None]] + within
    target_member = jnp.sum(
        (row_total[:, None, :] <= block_ids[None, :, None]).astype(jnp.int32), axis=2
    )
    target_member = jnp.minimum(target_member, replicas - 1)
    block_offset = block_ids[None, :] - row_start[member_ids[:, None], target_member]
    global_target = (
        target_member * capacity + column_start[member_ids[:, None], target_member] + block_offset
    )
    local_target = target_member * blocks_dev + block_offset
    return (
        wiring_section,
        row_start,
        column_start,
        slot_live,
        local_source,
        global_source,
        global_target,
        local_target,
    )


def gather_rows(local_rows):
    return lax.all_gather(local_rows, "rep", axis=0, tiled=True)


def reduce_rows(term_rows):
    return lax.psum_scatter(
        term_rows.astype(jnp.bfloat16), "rep", scatter_dimension=0, tiled=True
    ).astype(jnp.float32)


def route_blocks(buffer_rows):
    return lax.all_to_all(buffer_rows, "rep", split_axis=0, concat_axis=0, tiled=True)


def pass_section(slot_rows, offset_by):
    return passed_along(slot_rows, "section", offset_by)


def normalize(layer_rows, gain_row):
    values = layer_rows.astype(jnp.float32)
    row_scale = lax.rsqrt(jnp.mean(values * values, axis=1, keepdims=True) + epsilon)
    normed_local = (values * row_scale * gain_row[None, :]).astype(jnp.bfloat16)
    return (values, row_scale, gather_rows(normed_local))


def down_terms(hidden, down_local, values, position):
    term_rows = jnp.dot(hidden, down_local, preferred_element_type=jnp.float32)
    row_count = values.shape[0]
    own_part = lax.dynamic_slice_in_dim(term_rows, position * row_count, row_count, 0) + values
    return lax.dynamic_update_slice_in_dim(term_rows, own_part, position * row_count, 0)


def local_forward(layer_rows, gain_row, gate_local, up_local, down_local, position):
    values, row_scale, normed = normalize(layer_rows, gain_row)
    gate_act = jnp.dot(normed, gate_local, preferred_element_type=jnp.float32)
    up_act = jnp.dot(normed, up_local, preferred_element_type=jnp.float32)
    hidden = (jax.nn.silu(gate_act) * up_act).astype(jnp.bfloat16)
    term_rows = down_terms(hidden, down_local, values, position)
    return (term_rows, values, row_scale, normed, gate_act, up_act, hidden)


def values_rows_term(values, row_scale, scaled_grad):
    return values * row_scale**3 * jnp.mean(values * scaled_grad, axis=1, keepdims=True)


def per_device(layer_in, next_in, returned, norm_gain, gate_weight, up_weight, down_weight, wiring):
    replicas = lax.axis_size("rep")
    position = lax.axis_index("rep")
    partner_offset = lax.axis_size("section") // 2
    row_count = layer_in.shape[1]
    feature_count = layer_in.shape[2]
    blocks_dev = row_count // BLK
    capacity = returned.shape[1] // BLK
    token_count = row_count * replicas
    gain_row = norm_gain[0]
    gate_local = gate_weight[0]
    up_local = up_weight[0]
    down_local = down_weight[0]
    zero_value = jnp.zeros((), jnp.bfloat16)
    block_ids = jnp.arange(blocks_dev, dtype=jnp.int32)
    (
        counts,
        row_start,
        column_start,
        slot_live,
        local_source,
        global_source,
        global_target,
        local_target,
    ) = route_tables(wiring[0], replicas, blocks_dev, capacity)
    term_rows, values, row_scale, normed, gate_act, up_act, hidden = local_forward(
        layer_in[0], gain_row, gate_local, up_local, down_local, position
    )
    out_rows = reduce_rows(term_rows).astype(jnp.bfloat16)
    own_blocks = out_rows.reshape(blocks_dev, BLK, feature_count)
    my_start = lax.dynamic_index_in_dim(row_start, position, 0, keepdims=False)
    my_counts = lax.dynamic_index_in_dim(counts, position, 0, keepdims=False)
    pick_index = jnp.minimum(my_start[:, None] + block_ids[None, :], blocks_dev - 1)
    keep_mask = block_ids[None, :] < my_counts[:, None]
    outgoing = jnp.take(own_blocks, pick_index.reshape(-1), axis=0).reshape(
        replicas, blocks_dev, BLK, feature_count
    )
    outgoing = jnp.where(keep_mask[:, :, None, None], outgoing, zero_value)
    incoming = route_blocks(outgoing.reshape(replicas, row_count, feature_count))
    incoming = incoming.reshape(replicas * blocks_dev, BLK, feature_count)
    my_source = lax.dynamic_index_in_dim(local_source, position, 0, keepdims=False)
    my_live = lax.dynamic_index_in_dim(slot_live, position, 0, keepdims=False)
    slot_blocks = jnp.where(
        my_live[:, None, None], jnp.take(incoming, my_source, axis=0), zero_value
    )
    slot_rows = slot_blocks.reshape(capacity * BLK, feature_count)
    forwarded = pass_section(slot_rows, 1)
    later_slots = pass_section(returned[0], -1)
    back_blocks = later_slots.reshape(capacity, BLK, feature_count)
    column_offsets = lax.dynamic_index_in_dim(column_start, position, 1, keepdims=False)
    column_counts = lax.dynamic_index_in_dim(counts, position, 1, keepdims=False)
    pick_back = jnp.minimum(column_offsets[:, None] + block_ids[None, :], capacity - 1)
    keep_back = block_ids[None, :] < column_counts[:, None]
    returning = jnp.take(back_blocks, pick_back.reshape(-1), axis=0).reshape(
        replicas, blocks_dev, BLK, feature_count
    )
    returning = jnp.where(keep_back[:, :, None, None], returning, zero_value)
    arrived = route_blocks(returning.reshape(replicas, row_count, feature_count))
    arrived = arrived.reshape(replicas * blocks_dev, BLK, feature_count)
    my_target = lax.dynamic_index_in_dim(local_target, position, 0, keepdims=False)
    cotangent_own = jnp.take(arrived, my_target, axis=0).reshape(row_count, feature_count)
    cotangent_all = gather_rows(cotangent_own)
    rows_contract = (((0,), (0,)), ((), ()))
    cols_contract = (((1,), (1,)), ((), ()))
    update_factor = step_rate / token_count
    grad_down = lax.dot_general(
        hidden, cotangent_all, rows_contract, preferred_element_type=jnp.float32
    )
    updated_down = (down_local.astype(jnp.float32) - update_factor * grad_down).astype(jnp.bfloat16)
    mate_down = passed_along(updated_down, "section", partner_offset)
    dhidden = lax.dot_general(
        cotangent_all, down_local, cols_contract, preferred_element_type=jnp.float32
    )
    sigmoid_gate = jax.nn.sigmoid(gate_act)
    silu_gate = gate_act * sigmoid_gate
    grad_gate_act = (
        dhidden * up_act * sigmoid_gate * (1.0 + gate_act * (1.0 - sigmoid_gate))
    ).astype(jnp.bfloat16)
    grad_up_act = (dhidden * silu_gate).astype(jnp.bfloat16)
    dterm_rows = lax.dot_general(
        grad_gate_act, gate_local, cols_contract, preferred_element_type=jnp.float32
    )
    dterm_rows = dterm_rows + lax.dot_general(
        grad_up_act, up_local, cols_contract, preferred_element_type=jnp.float32
    )
    dnormed = reduce_rows(dterm_rows)
    scaled_grad = gain_row[None, :] * dnormed
    input_grad = (
        cotangent_own.astype(jnp.float32)
        + row_scale * scaled_grad
        - values_rows_term(values, row_scale, scaled_grad)
    ).astype(jnp.bfloat16)
    grad_gate = lax.dot_general(
        normed, grad_gate_act, rows_contract, preferred_element_type=jnp.float32
    )
    grad_up = lax.dot_general(
        normed, grad_up_act, rows_contract, preferred_element_type=jnp.float32
    )
    updated_gate = (gate_local.astype(jnp.float32) - update_factor * grad_gate).astype(jnp.bfloat16)
    updated_up = (up_local.astype(jnp.float32) - update_factor * grad_up).astype(jnp.bfloat16)
    next_values, next_scale, next_normed = normalize(next_in[0], gain_row)
    own_gate_next = jnp.dot(next_normed, updated_gate, preferred_element_type=jnp.float32)
    own_up_next = jnp.dot(next_normed, updated_up, preferred_element_type=jnp.float32)
    mate_pair = passed_along(jnp.stack((updated_gate, updated_up)), "section", partner_offset)
    mate_gate_next = jnp.dot(next_normed, mate_pair[0], preferred_element_type=jnp.float32)
    mate_up_next = jnp.dot(next_normed, mate_pair[1], preferred_element_type=jnp.float32)
    gate_next = 0.5 * (own_gate_next + mate_gate_next)
    up_next = 0.5 * (own_up_next + mate_up_next)
    hidden_next = (jax.nn.silu(gate_next) * up_next).astype(jnp.bfloat16)
    averaged_down = (
        (updated_down.astype(jnp.float32) + mate_down.astype(jnp.float32)) * 0.5
    ).astype(jnp.bfloat16)
    term_next = down_terms(hidden_next, averaged_down, next_values, position)
    next_rows = reduce_rows(term_next).astype(jnp.bfloat16)
    return (forwarded[None], input_grad[None], next_rows[None])


def solution(mesh):
    in_specs = (
        P("section", "rep", None),
        P("section", "rep", None),
        P("section", "rep", None),
        P("section", None),
        P("section", None, "rep"),
        P("section", None, "rep"),
        P("section", "rep", None),
        P("section", None, None),
    )
    out_specs = (P("section", "rep", None), P("section", "rep", None), P("section", "rep", None))
    return jax.shard_map(
        per_device, mesh=mesh, in_specs=in_specs, out_specs=out_specs, check_vma=False
    )
```

profile of v0, /device:TPU:33, one launch (start us, length us, event | category | flops | bytes accessed | tf_op | source)
XLA Modules:
  0.0 1053.8 jit_solution(2265218487439478688)
XLA Ops:
  7.2 8.3 collective-permute-start.1
  15.4 0.8 reduce_window_sum.22
  16.2 0.9 reduce_window_sum.23
  17.1 0.9 dynamic-slice_reduce_fusion.1
  18.0 0.7 bitcast_subtract_fusion
  19.5 0.9 fusion.27
  20.4 0.9 fusion.23
  21.4 2.7 gather_fusion.4
  24.1 0.4 gather.37
  24.5 1.8 select_select_fusion
  26.3 7.6 all-to-all-start.1
  34.0 0.7 fusion.36
  35.1 0.8 gather_fusion.3
  36.5 24.2 %all-to-all-done.1 = bf16[32,4,4096]{2,1,0:T(4,128)(2,1)S(1)} async-done(((bf16[32,4,4096]{2,1,0:T(4,128)(2,1)}), bf16[32,4,4096]{2,1,0:T(4,128)(2,1)S(1)}, u32[]{:S(2)}, u32[]{:S(2)}) %all-to-all-start.1) | async-done | bytes 1048608 | tf_op jit(solution)/shard_map/all_to_all | solution.py:65
  60.7 0.5 reshape.323
  61.2 0.6 gather_fusion.5
  61.9 0.7 fusion.55
  62.6 0.2 all-gather.11.cloned.1.call-start
  62.8 32.1 %all-gather.7.cloned.1.call-done = bf16[32,4,4096]{2,1,0:T(4,128)(2,1)} async-done(((bf16[1,4,4096]{2,1,0:T(4,128)(2,1)}), bf16[32,4,4096]{2,1,0:T(4,128)(2,1)}) %all-gather.7.cloned.1.call-update) | async-done | bytes 1048592 | tf_op jit(solution)/shard_map/all_gather | solution.py:55
  95.0 1.3 reshape.371
  96.3 3.3 fusion.13
  99.6 1.1 fusion.9
  100.8 53.6 %all-gather.9.cloned.1.call-done = bf16[32,4,4096]{2,1,0:T(4,128)(2,1)} async-done(((bf16[1,4,4096]{2,1,0:T(4,128)(2,1)}), bf16[32,4,4096]{2,1,0:T(4,128)(2,1)}) %all-gather.9.cloned.1.call-update) | async-done | bytes 1048592 | tf_op jit(solution)/shard_map/all_gather | solution.py:55
  154.4 1.3 reshape.373
  155.7 3.3 multiply_convert_fusion.3
  159.1 1.1 subtract_convert_fusion.2
  160.2 0.9 copy-done.7
  161.1 1.1 subtract_convert_fusion.1
  162.2 4.0 pad_maximum_fusion
  166.4 3.7 collective-permute-start.2
  170.1 4.9 subtract_convert_fusion
  175.0 1.7 collective-permute-start.3
  176.7 508.5 %all-gather.11.cloned.1.call-done = bf16[32,4,4096]{2,1,0:T(4,128)(2,1)} async-done(((bf16[1,4,4096]{2,1,0:T(4,128)(2,1)}), bf16[32,4,4096]{2,1,0:T(4,128)(2,1)}) %all-gather.11.cloned.1.call-update) | async-done | bytes 1048592 | tf_op jit(solution)/shard_map/all_gather | solution.py:55
  685.2 1.3 reshape.375
  686.6 2.9 fusion.6
  689.6 1.2 convert_element_type.90
  690.7 1.1 fusion.56
  692.0 1.1 fusion.57
  693.1 0.9 copy-done.5
  694.1 0.8 fusion.11
  694.8 1.3 copy-done.8
  696.1 1.8 fusion
  697.9 3.9 fusion.17
  701.7 6.9 fusion.1
  708.7 1.1 convert_element_type.111
  710.1 0.7 fusion.47
  711.4 1.3 gather_fusion
  712.9 0.6 dynamic-slice.2
  714.2 260.7 %all-reduce.6.cloned.1.call-done = (bf16[128,4096]{1,0:T(8,128)(2,1)}, bf16[128,4096]{1,0:T(8,128)(2,1)}, bf16[128,4096]{1,0:T(8,128)(2,1)}) async-done(((bf16[128,4096]{1,0:T(8,128)(2,1)}, bf16[128,4096]{1,0:T(8,128)(2,1)}, bf16[128,4096]{1,0:T(8,128)(2,1)}), (bf16[128,4096]{1,0:T(8,128)(2,1)}, bf16[128,4096]{1,0:T(8,128)(2,1)}, bf16[128,4096]{1,0:T(8,128)(2,1)})) %all-reduce.6.cloned.1.call-update) | async-done | bytes 3145744
  974.9 0.9 constant_dynamic-slice_fusion.5
  975.8 2.7 gather_fusion.1
  978.4 0.4 gather.32
  978.9 1.7 select_select_fusion.1
  980.6 27.0 %all-to-all-start = ((bf16[32,4,4096]{2,1,0:T(4,128)(2,1)}), bf16[32,4,4096]{2,1,0:T(4,128)(2,1)S(1)}, u32[]{:S(2)}, u32[]{:S(2)}) async-start(bf16[32,4,4096]{2,1,0:T(4,128)(2,1)} %select_select_fusion.1), calls=%async_computation | async-start | bytes 2097152 | tf_op jit(solution)/shard_map/all_to_all | solution.py:65
  1008.0 0.2 fusion.42
  1008.4 1.0 fusion.34
  1009.4 1.6 fusion.37
  1010.9 23.4 %all-to-all-done = bf16[32,4,4096]{2,1,0:T(4,128)(2,1)S(1)} async-done(((bf16[32,4,4096]{2,1,0:T(4,128)(2,1)}), bf16[32,4,4096]{2,1,0:T(4,128)(2,1)S(1)}, u32[]{:S(2)}, u32[]{:S(2)}) %all-to-all-start) | async-done | bytes 1048608 | tf_op jit(solution)/shard_map/all_to_all | solution.py:65
  1034.4 0.5 reshape.321
  1034.9 0.7 gather_fusion.2
  1035.7 1.3 collective-permute-start
  1037.0 1.5 dynamic-slice_bitcast_fusion
  1038.5 8.2 collective-permute-done
  1046.6 0.6 copy.72
  (101 shorter events, 4.0 us)
Async XLA Ops:
  7.2 14.2 %collective-permute-start.1 = (bf16[8,4096]{1,0:T(8,128)(2,1)}, bf16[8,4096]{1,0:T(8,128)(2,1)S(1)}, u32[]{:S(2)}, u32[]{:S(2)}) collective-permute-start(bf16[8,4096]{1,0:T(8,128)(2,1)} %bitcast.133), channel_id=1, source_target_pairs={{0,224},{32,0},{64,32},{96,64},{128,96},{160,128},{192,160},{224,1... | collective-permute-start | bytes 196616 | tf_op jit(solution)/shard_map/ppermute | solution.py:13
  24.0 9.9 copy-start.9
  24.1 9.9 copy-start.10
  24.1 9.9 copy-start.11
  26.3 34.4 %all-to-all-start.1 = ((bf16[32,4,4096]{2,1,0:T(4,128)(2,1)}), bf16[32,4,4096]{2,1,0:T(4,128)(2,1)S(1)}, u32[]{:S(2)}, u32[]{:S(2)}) async-start(bf16[32,4,4096]{2,1,0:T(4,128)(2,1)} %select_select_fusion), calls=%async_computation.1 | async-start | bytes 2097152 | tf_op jit(solution)/shard_map/all_to_all | solution.py:65
  33.9 61.1 %all-gather.7.cloned.1.call-start = ((), (), s32[]{:S(2)}) async-start(), calls=%async_computation.2 | async-start | bytes 1081344 | tf_op jit(solution)/shard_map/all_gather | solution.py:55
  34.7 119.7 %all-gather.9.cloned.1.call-start = ((), (), s32[]{:S(2)}) async-start(), calls=%async_computation.3 | async-start | bytes 1081344 | tf_op jit(solution)/shard_map/all_gather | solution.py:55
  62.6 622.6 %all-gather.11.cloned.1.call-start = ((), (), s32[]{:S(2)}) async-start(), calls=%async_computation.4 | async-start | bytes 1081344 | tf_op jit(solution)/shard_map/all_gather | solution.py:55
  96.3 3.3 copy-start.6
  155.7 3.3 copy-start.4
  159.1 2.0 copy-start.7
  160.2 2.0 copy-start.2
  162.2 4.1 copy-start
  166.4 531.5 %collective-permute-start.2 = (bf16[2,4096,448]{1,2,0:T(8,128)(2,1)}, bf16[2,4096,448]{1,2,0:T(8,128)(2,1)}, u32[]{:S(2)}, u32[]{:S(2)}) collective-permute-start(bf16[2,4096,448]{1,2,0:T(8,128)(2,1)} %pad_maximum_fusion), channel_id=1, source_target_pairs={{0,128},{32,160},{64,192},{96,224},{128,0},{160,32},{192,64},{224,... | collective-permute-start | bytes 22020104 | tf_op jit(solution)/shard_map/ppermute | solution.py:13
  170.0 804.8 %all-reduce.6.cloned.1.call-start = ((), (), s32[]{:S(2)}) async-start(), calls=%async_computation.5 | async-start | bytes 6291456
  175.0 526.7 %collective-permute-start.3 = (bf16[448,4096]{1,0:T(8,128)(2,1)}, bf16[448,4096]{1,0:T(8,128)(2,1)}, u32[]{:S(2)}, u32[]{:S(2)}) collective-permute-start(bf16[448,4096]{1,0:T(8,128)(2,1)} %subtract_convert_fusion), channel_id=1, source_target_pairs={{0,128},{32,160},{64,192},{96,224},{128,0},{160,32},{192,64},{224,... | collective-permute-start | bytes 11010056 | tf_op jit(solution)/shard_map/ppermute | solution.py:13
  686.6 4.2 copy-start.3
  689.6 2.5 copy-start.1
  692.0 2.0 copy-start.5
  694.1 2.0 copy-start.8
  711.4 1.5 copy-start.12
  980.6 53.8 %all-to-all-start = ((bf16[32,4,4096]{2,1,0:T(4,128)(2,1)}), bf16[32,4,4096]{2,1,0:T(4,128)(2,1)S(1)}, u32[]{:S(2)}, u32[]{:S(2)}) async-start(bf16[32,4,4096]{2,1,0:T(4,128)(2,1)} %select_select_fusion.1), calls=%async_computation | async-start | bytes 2097152 | tf_op jit(solution)/shard_map/all_to_all | solution.py:65
  1035.7 10.9 %collective-permute-start = (bf16[8,4096]{1,0:T(8,128)(2,1)S(1)}, bf16[8,4096]{1,0:T(8,128)(2,1)S(1)}, u32[]{:S(2)}, u32[]{:S(2)}) collective-permute-start(bf16[8,4096]{1,0:T(8,128)(2,1)S(1)} %select_select_fusion.2), channel_id=1, source_target_pairs={{0,32},{32,64},{64,96},{96,128},{128,160},{160,192},{192,224},{224... | collective-permute-start | bytes 196616 | tf_op jit(solution)/shard_map/ppermute | solution.py:13
Sparse Core Ops, SparseCore 0:
  37.2 57.7 all-gather.6
  97.4 56.9 all-gather.8
  170.2 515.0 all-gather.10
  709.9 264.9 all-reduce.5
where the time goes:
time: 1050 us
  waiting for transfers between devices  911 us (87%)
  starting transfers between devices  49.9 us (5%)
  matrix products  33.3 us (3%)
  local copies, waits for them, and re-layouts  26.3 us (3%)
  other arithmetic  18.6 us (2%)
  between operations  14.9 us (1%)
    all_gather x3, waiting for transfers between devices, gather_rows(): return lax.all_gather(local_rows, 'rep', axis=0, tiled=True)  594 us
    unnamed x5, waiting for transfers between devices  261 us
    all_to_all x2, waiting for transfers between devices, route_blocks(): lax.all_to_all(buffer_rows, 'rep', split_axis=0, concat_axis=0, tiled=True)  47.6 us
    all_to_all x2, starting transfers between devices, route_blocks(): lax.all_to_all(buffer_rows, 'rep', split_axis=0, concat_axis=0, tiled=True)  34.6 us
  transfers between devices with their start and end apart: 10, of which 7 were waited for; matrix products, arithmetic and copies ran while one was open for 4% of the time, Pallas kernels for 0%

commit v1 on v0

--- a/solution.py
+++ b/solution.py
@@ -52,7 +52,9 @@
 
 
 def gather_rows(local_rows):
-    return lax.all_gather(local_rows, "rep", axis=0, tiled=True)
+    return jnp.concatenate(
+        lax.all_to_all(jnp.stack([local_rows] * lax.axis_size("rep")), "rep", 0, 0), axis=0
+    )
 
 
 def reduce_rows(term_rows):

time: 1050 us -> 1000 us (0.952)
  waiting for transfers between devices: 911 us -> 844 us
  starting transfers between devices: 49.9 us -> 65 us
    all_gather x3 -> x0, waiting for transfers between devices: 594 us -> none  [gather_rows(): return lax.all_gather(local_rows, 'rep', axis=0, tiled=True)]
    all_to_all x0 -> x3, waiting for transfers between devices: none -> 526 us  [gather_rows(): lax.all_to_all(jnp.stack([local_rows] * lax.axis_size('rep')), 'rep', 0, 0)]
    all_to_all x0 -> x3, starting transfers between devices: none -> 15.4 us  [gather_rows(): lax.all_to_all(jnp.stack([local_rows] * lax.axis_size('rep')), 'rep', 0, 0)]
    unnamed x5 -> x2, waiting for transfers between devices: 261 us -> 260 us
where the time goes in v1:
time: 1000 us
  waiting for transfers between devices  844 us (84%)
  starting transfers between devices  65 us (6%)
  matrix products  35.1 us (4%)
  local copies, waits for them, and re-layouts  27.6 us (3%)
  other arithmetic  15.8 us (2%)
  between operations  15.2 us (2%)
    all_to_all x3, waiting for transfers between devices, gather_rows(): lax.all_to_all(jnp.stack([local_rows] * lax.axis_size('rep')), 'rep', 0, 0)  526 us
    unnamed x2, waiting for transfers between devices  260 us
    all_to_all x2, waiting for transfers between devices, route_blocks(): lax.all_to_all(buffer_rows, 'rep', split_axis=0, concat_axis=0, tiled=True)  49.8 us
    all_to_all x2, starting transfers between devices, route_blocks(): lax.all_to_all(buffer_rows, 'rep', split_axis=0, concat_axis=0, tiled=True)  34.6 us
  transfers between devices with their start and end apart: 10, of which 7 were waited for; matrix products, arithmetic and copies ran while one was open for 4% of the time, Pallas kernels for 0%

profile of v1, /device:TPU:33, one launch (start us, length us, event | category | flops | bytes accessed | tf_op | source)
XLA Modules:
  0.0 1002.9 jit_solution(122088677672634447)
XLA Ops:
  7.2 8.3 collective-permute-start.1
  15.4 0.8 reduce_window_sum.22
  16.2 0.9 reduce_window_sum.23
  17.1 0.9 dynamic-slice_reduce_fusion.1
  18.0 0.7 bitcast_subtract_fusion
  19.5 2.7 gather_fusion.4
  22.2 0.4 gather.37
  22.7 1.7 select_select_fusion
  24.4 7.6 all-to-all-start.2
  32.5 26.3 %all-to-all-done.2 = bf16[32,4,4096]{2,1,0:T(4,128)(2,1)S(1)} async-done(((bf16[32,4,4096]{2,1,0:T(4,128)(2,1)}), bf16[32,4,4096]{2,1,0:T(4,128)(2,1)S(1)}, u32[]{:S(2)}, u32[]{:S(2)}) %all-to-all-start.2) | async-done | bytes 1048608 | tf_op jit(solution)/shard_map/all_to_all | solution.py:67
  58.8 1.5 stack.17
  60.3 5.0 all-to-all-start
  65.6 0.8 gather_fusion.3
  67.0 0.6 reshape.365
  67.6 0.6 gather_fusion.5
  68.3 23.7 %all-to-all-done = bf16[32,4,4096]{2,1,0:T(4,128)(2,1)S(1)} async-done(((bf16[32,4,4096]{2,1,0:T(4,128)(2,1)}), bf16[32,4,4096]{2,1,0:T(4,128)(2,1)S(1)}, u32[]{:S(2)}, u32[]{:S(2)}) %all-to-all-start) | async-done | bytes 1048608 | tf_op jit(solution)/shard_map/all_to_all | solution.py:56
  92.1 1.5 stack.18
  93.5 5.1 all-to-all-start.3
  98.6 0.3 reshape.361
  98.9 4.0 fusion.13
  102.9 1.8 fusion.9
  104.7 20.6 %all-to-all-done.3 = bf16[32,4,4096]{2,1,0:T(4,128)(2,1)S(1)} async-done(((bf16[32,4,4096]{2,1,0:T(4,128)(2,1)}), bf16[32,4,4096]{2,1,0:T(4,128)(2,1)S(1)}, u32[]{:S(2)}, u32[]{:S(2)}) %all-to-all-start.3) | async-done | bytes 1048608 | tf_op jit(solution)/shard_map/all_to_all | solution.py:56
  125.3 0.3 reshape.366
  125.6 3.7 multiply_convert_fusion.3
  129.4 1.1 subtract_convert_fusion.2
  130.5 0.9 copy-done.7
  131.4 1.1 subtract_convert_fusion.1
  132.5 4.0 pad_maximum_fusion
  136.6 1.2 collective-permute-start.2
  137.8 1.5 stack.20
  139.3 5.3 all-to-all-start.4
  144.7 4.9 subtract_convert_fusion
  149.6 4.2 collective-permute-start.3
  153.8 481.6 %all-to-all-done.4 = bf16[32,4,4096]{2,1,0:T(4,128)(2,1)S(1)} async-done(((bf16[32,4,4096]{2,1,0:T(4,128)(2,1)}), bf16[32,4,4096]{2,1,0:T(4,128)(2,1)S(1)}, u32[]{:S(2)}, u32[]{:S(2)}) %all-to-all-start.4) | async-done | bytes 1048608 | tf_op jit(solution)/shard_map/all_to_all | solution.py:56
  635.4 0.3 reshape.367
  635.7 2.9 fusion.6
  638.7 1.2 convert_element_type.99
  639.9 1.1 fusion.61
  641.1 1.1 fusion.62
  642.3 0.9 copy-done.5
  643.2 0.8 fusion.11
  643.9 1.3 copy-done.8
  645.2 1.8 fusion
  647.0 3.9 fusion.17
  650.9 6.9 fusion.1
  657.8 1.1 convert_element_type.121
  659.3 0.7 fusion.53
  660.5 1.3 gather_fusion
  662.0 0.6 dynamic-slice.2
  663.3 260.3 %all-reduce.6.cloned.1.call-done = (bf16[128,4096]{1,0:T(8,128)(2,1)}, bf16[128,4096]{1,0:T(8,128)(2,1)}, bf16[128,4096]{1,0:T(8,128)(2,1)}) async-done(((bf16[128,4096]{1,0:T(8,128)(2,1)}, bf16[128,4096]{1,0:T(8,128)(2,1)}, bf16[128,4096]{1,0:T(8,128)(2,1)}), (bf16[128,4096]{1,0:T(8,128)(2,1)}, bf16[128,4096]{1,0:T(8,128)(2,1)}, bf16[128,4096]{1,0:T(8,128)(2,1)})) %all-reduce.6.cloned.1.call-update) | async-done | bytes 3145744
  923.6 0.9 constant_dynamic-slice_fusion.5
  924.5 2.7 gather_fusion.1
  927.2 0.4 gather.32
  927.6 1.7 select_select_fusion.1
  929.4 27.0 %all-to-all-start.1 = ((bf16[32,4,4096]{2,1,0:T(4,128)(2,1)}), bf16[32,4,4096]{2,1,0:T(4,128)(2,1)S(1)}, u32[]{:S(2)}, u32[]{:S(2)}) async-start(bf16[32,4,4096]{2,1,0:T(4,128)(2,1)} %select_select_fusion.1), calls=%async_computation.1 | async-start | bytes 2097152 | tf_op jit(solution)/shard_map/all_to_all | solution.py:67
  957.1 1.0 fusion.34
  958.1 1.6 fusion.43
  959.7 23.4 %all-to-all-done.1 = bf16[32,4,4096]{2,1,0:T(4,128)(2,1)S(1)} async-done(((bf16[32,4,4096]{2,1,0:T(4,128)(2,1)}), bf16[32,4,4096]{2,1,0:T(4,128)(2,1)S(1)}, u32[]{:S(2)}, u32[]{:S(2)}) %all-to-all-start.1) | async-done | bytes 1048608 | tf_op jit(solution)/shard_map/all_to_all | solution.py:67
  983.1 0.5 reshape.363
  983.7 0.7 gather_fusion.2
  984.5 1.3 collective-permute-start
  985.7 1.5 dynamic-slice_bitcast_fusion
  987.2 8.2 collective-permute-done
  995.4 0.6 copy.72
  (104 shorter events, 4.6 us)
Async XLA Ops:
  7.2 12.3 %collective-permute-start.1 = (bf16[8,4096]{1,0:T(8,128)(2,1)}, bf16[8,4096]{1,0:T(8,128)(2,1)S(1)}, u32[]{:S(2)}, u32[]{:S(2)}) collective-permute-start(bf16[8,4096]{1,0:T(8,128)(2,1)} %bitcast.151), channel_id=1, source_target_pairs={{0,224},{32,0},{64,32},{96,64},{128,96},{160,128},{192,160},{224,1... | collective-permute-start | bytes 196616 | tf_op jit(solution)/shard_map/ppermute | solution.py:13
  22.2 9.8 copy-start.11
  22.2 10.0 copy-start.12
  22.2 10.1 %copy-start.13 = (f32[1,4096]{1,0:T(1,128)S(1)}, f32[1,4096]{1,0:T(1,128)}, u32[]{:S(2)}) copy-start(f32[1,4096]{1,0:T(1,128)} %param.11) | copy-start | bytes 49156
  24.4 34.4 %all-to-all-start.2 = ((bf16[32,4,4096]{2,1,0:T(4,128)(2,1)}), bf16[32,4,4096]{2,1,0:T(4,128)(2,1)S(1)}, u32[]{:S(2)}, u32[]{:S(2)}) async-start(bf16[32,4,4096]{2,1,0:T(4,128)(2,1)} %select_select_fusion), calls=%async_computation.2 | async-start | bytes 2097152 | tf_op jit(solution)/shard_map/all_to_all | solution.py:67
  60.3 31.8 %all-to-all-start = ((bf16[32,4,4096]{2,1,0:T(4,128)(2,1)}), bf16[32,4,4096]{2,1,0:T(4,128)(2,1)S(1)}, u32[]{:S(2)}, u32[]{:S(2)}) async-start(bf16[32,4,4096]{2,1,0:T(4,128)(2,1)} %stack.17), calls=%async_computation | async-start | bytes 2097152 | tf_op jit(solution)/shard_map/all_to_all | solution.py:56
  93.5 31.8 %all-to-all-start.3 = ((bf16[32,4,4096]{2,1,0:T(4,128)(2,1)}), bf16[32,4,4096]{2,1,0:T(4,128)(2,1)S(1)}, u32[]{:S(2)}, u32[]{:S(2)}) async-start(bf16[32,4,4096]{2,1,0:T(4,128)(2,1)} %stack.18), calls=%async_computation.3 | async-start | bytes 2097152 | tf_op jit(solution)/shard_map/all_to_all | solution.py:56
  98.9 4.0 copy-start.6
  125.6 4.9 copy-start.9
  125.6 3.7 copy-start.4
  129.3 2.0 copy-start.7
  130.5 2.0 copy-start.2
  132.5 4.1 copy-start
  136.6 8.0 copy-start.10
  136.6 510.4 %collective-permute-start.2 = (bf16[2,4096,448]{1,2,0:T(8,128)(2,1)}, bf16[2,4096,448]{1,2,0:T(8,128)(2,1)}, u32[]{:S(2)}, u32[]{:S(2)}) collective-permute-start(bf16[2,4096,448]{1,2,0:T(8,128)(2,1)} %pad_maximum_fusion), channel_id=1, source_target_pairs={{0,128},{32,160},{64,192},{96,224},{128,0},{160,32},{192,64},{224,... | collective-permute-start | bytes 22020104 | tf_op jit(solution)/shard_map/ppermute | solution.py:13
  139.3 496.1 %all-to-all-start.4 = ((bf16[32,4,4096]{2,1,0:T(4,128)(2,1)}), bf16[32,4,4096]{2,1,0:T(4,128)(2,1)S(1)}, u32[]{:S(2)}, u32[]{:S(2)}) async-start(bf16[32,4,4096]{2,1,0:T(4,128)(2,1)} %stack.20), calls=%async_computation.4 | async-start | bytes 2097152 | tf_op jit(solution)/shard_map/all_to_all | solution.py:56
  144.6 779.0 %all-reduce.6.cloned.1.call-start = ((), (), s32[]{:S(2)}) async-start(), calls=%async_computation.5 | async-start | bytes 6291456
  149.6 501.2 %collective-permute-start.3 = (bf16[448,4096]{1,0:T(8,128)(2,1)}, bf16[448,4096]{1,0:T(8,128)(2,1)}, u32[]{:S(2)}, u32[]{:S(2)}) collective-permute-start(bf16[448,4096]{1,0:T(8,128)(2,1)} %subtract_convert_fusion), channel_id=1, source_target_pairs={{0,128},{32,160},{64,192},{96,224},{128,0},{160,32},{192,64},{224,... | collective-permute-start | bytes 11010056 | tf_op jit(solution)/shard_map/ppermute | solution.py:13
  635.7 4.2 copy-start.3
  638.7 2.5 copy-start.1
  641.1 2.0 copy-start.5
  643.2 2.0 copy-start.8
  660.5 1.5 copy-start.14
  929.4 53.8 %all-to-all-start.1 = ((bf16[32,4,4096]{2,1,0:T(4,128)(2,1)}), bf16[32,4,4096]{2,1,0:T(4,128)(2,1)S(1)}, u32[]{:S(2)}, u32[]{:S(2)}) async-start(bf16[32,4,4096]{2,1,0:T(4,128)(2,1)} %select_select_fusion.1), calls=%async_computation.1 | async-start | bytes 2097152 | tf_op jit(solution)/shard_map/all_to_all | solution.py:67
  984.5 10.9 %collective-permute-start = (bf16[8,4096]{1,0:T(8,128)(2,1)S(1)}, bf16[8,4096]{1,0:T(8,128)(2,1)S(1)}, u32[]{:S(2)}, u32[]{:S(2)}) collective-permute-start(bf16[8,4096]{1,0:T(8,128)(2,1)S(1)} %select_select_fusion.2), channel_id=1, source_target_pairs={{0,32},{32,64},{64,96},{96,128},{128,160},{160,192},{192,224},{224... | collective-permute-start | bytes 196616 | tf_op jit(solution)/shard_map/ppermute | solution.py:13
Sparse Core Ops, SparseCore 0:
  659.0 264.5 all-reduce.5
